TPU v7x, 1024 devices: a whole 8x8x8 slice. The times are simulated.
1024 devices in a mesh: group: 64 (over z_hi, y, core), head: 16 (over z_lo, x).
Axes of the slice: x: 8, y: 8, z: 8 (z_hi: 4, z_lo: 2; z = z_hi * 2 + z_lo), core: 2. Of those that a mesh axis runs over, the one named last changes fastest.
Arguments:
- key_grad: bfloat16 [32768, 16384], P('group', 'head'), may hold values from -16 to 16
- value_grad: bfloat16 [32768, 16384], P('group', 'head'), may hold values from -6 to 6
- rope_grad: bfloat16 [32768, 8192], P('group', 'head'), may hold values from -1.5 to 1.5
- key_lift: bfloat16 [512, 16384], P(None, 'head'), may hold values from -0.046875 to 0.046875
- value_lift: bfloat16 [512, 16384], P(None, 'head'), may hold values from -0.046875 to 0.046875
- latent: bfloat16 [32768, 512], P('group'), may hold values from -40 to 40
- norm_gain: float32 [512], replicated, may hold values from 0.25 to 1.75
- doc_lengths: int32 [64, 4], P('group'), may hold values from 1 to 256, 512 in all within a row
- hidden: bfloat16 [32768, 7168], P('group', 'head'), may hold values from -0.078125 to 0.078125
- down_proj: bfloat16 [7168, 576], P('head'), may hold values from -0.0625 to 0.0625
Outputs:
- hidden_grad: bfloat16 [32768, 7168], P('group', 'head')
- weight_grad: float32 [576, 7168], P('group', 'head')
Inputs may be any that keep to these rules, and one draw needn't show every extreme that they name: `doc_lengths`: each row sums to 512 and its largest entry is 256.
All inputs are finite; a program needn't handle non-finite values.
Results may differ from a plain program's by a relative error of at most 0.0049.
Values may be sent and summed in bfloat16 or wider, within the bound.
A program may use at most 32 MiB of HBM per device.

v0:
```python
import jax
import jax.numpy as jnp
from jax import lax
from jax.sharding import PartitionSpec as P

LATENT = 512
ROPE = 64


def positions(lengths, token_index):
    doc_ends = jnp.cumsum(lengths, axis=1)
    doc_start = jnp.max(jnp.where(doc_ends <= token_index[:, None], doc_ends, 0), axis=1)
    return token_index - doc_start


def kva_rows_grad(stacked, latent, norm_gain, position):
    latent_part = stacked[:, :LATENT]
    rotary_part = stacked[:, LATENT:]
    values = latent.astype(jnp.float32)
    inverse_rms = lax.rsqrt(jnp.mean(values * values, axis=1, keepdims=True) + 1e-06)
    scaled_grad = latent_part * norm_gain[None, :]
    norm_grad = inverse_rms * (
        scaled_grad
        - values * inverse_rms * inverse_rms * jnp.mean(scaled_grad * values, axis=1, keepdims=True)
    )
    half_width = rotary_part.shape[1] // 2
    inv_freq = 10000.0 ** (-(2.0 * jnp.arange(half_width, dtype=jnp.float32)) / (2.0 * half_width))
    angles = position.astype(jnp.float32)[:, None] * inv_freq[None, :]
    cosine = jnp.cos(angles)
    sine = jnp.sin(angles)
    first_half = rotary_part[:, :half_width]
    second_half = rotary_part[:, half_width:]
    rot_first = first_half * cosine + second_half * sine
    rot_second = second_half * cosine - first_half * sine
    return jnp.concatenate([norm_grad, rot_first, rot_second], axis=1).astype(jnp.bfloat16)


def on_device(
    key_grad,
    value_grad,
    rope_grad,
    key_lift,
    value_lift,
    latent,
    norm_gain,
    doc_lengths,
    hidden,
    down_proj,
):
    contract = (((1,), (1,)), ((), ()))
    seq_len = key_grad.shape[0]
    head_terms = lax.dot_general(key_grad, key_lift, contract, preferred_element_type=jnp.float32)
    head_terms = head_terms + lax.dot_general(
        value_grad, value_lift, contract, preferred_element_type=jnp.float32
    )
    heads_here = rope_grad.shape[1] // ROPE
    rope_terms = jnp.sum(rope_grad.reshape(seq_len, heads_here, ROPE), axis=1, dtype=jnp.float32)
    stacked = jnp.concatenate([head_terms, rope_terms], axis=1)
    shared = lax.psum_scatter(stacked, "head", scatter_dimension=0, tiled=True)
    share_rows = shared.shape[0]
    first_row = lax.axis_index("head") * share_rows
    own_latent = lax.dynamic_slice_in_dim(latent, first_row, share_rows, 0)
    token_index = first_row + jnp.arange(share_rows, dtype=jnp.int32)
    row_lengths = jnp.broadcast_to(doc_lengths, (share_rows, doc_lengths.shape[1]))
    own_grad = kva_rows_grad(shared, own_latent, norm_gain, positions(row_lengths, token_index))
    kva_grad = lax.all_gather(own_grad, "head", axis=0, tiled=True)
    hidden_grad = lax.dot_general(
        kva_grad, down_proj, contract, preferred_element_type=jnp.float32
    ).astype(jnp.bfloat16)
    weight_grad = lax.psum_scatter(
        lax.dot_general(
            kva_grad, hidden, (((0,), (0,)), ((), ())), preferred_element_type=jnp.float32
        ),
        "group",
        scatter_dimension=0,
        tiled=True,
    )
    return (hidden_grad, weight_grad)


def solution(mesh):
    return jax.shard_map(
        on_device,
        mesh=mesh,
        in_specs=(
            P("group", "head"),
            P("group", "head"),
            P("group", "head"),
            P(None, "head"),
            P(None, "head"),
            P("group", None),
            P(),
            P("group", None),
            P("group", "head"),
            P("head", None),
        ),
        out_specs=(P("group", "head"), P("group", "head")),
        check_vma=False,
    )
```

profile of v0, /device:TPU:1, one launch (start us, length us, event | category | flops | bytes accessed | tf_op | source)
XLA Modules:
  0.0 695.6 jit_solution(6074644147892411792)
XLA Ops:
  7.2 1.4 copy.25
  8.7 0.2 copy-done.6
  8.9 0.7 fusion.17
  9.6 0.5 copy-done.1
  10.1 0.3 copy-done.2
  10.4 0.7 convolution_add_fusion
  11.2 0.1 pad_maximum_fusion
  11.2 1.5 copy.29
  12.8 0.6 copy-done.5
  13.5 78.8 %reduce-scatter.4.cloned.1.call-done = f32[32,576]{1,0:T(8,128)} async-done(((f32[512,576]{1,0:T(8,128)}), f32[32,576]{1,0:T(8,128)}) %reduce-scatter.4.cloned.1.call-update) | async-done | bytes 73744 | tf_op jit(solution)/shard_map/reduce_scatter | solution.py:59
  92.3 0.9 fusion.16
  93.2 0.1 copy.32
  93.4 0.2 fusion.12
  93.5 0.1 copy.28
  93.6 0.1 copy.27
  93.7 1.0 fusion
  94.7 0.9 fusion.5
  95.6 0.1 pad_maximum_fusion.1
  95.7 27.4 %all_gather.3 = bf16[512,576]{1,0:T(8,128)(2,1)S(1)} all-gather(bf16[32,576]{1,0:T(8,128)(2,1)S(1)} %pad_maximum_fusion.1), channel_id=1, replica_groups=mesh['group'=64,'head'=16] {'head'}, dimensions={0}, use_global_device_ids=true | all-gather | bytes 626688 | tf_op jit(solution)/shard_map/all_gather | solution.py:66
  123.1 1.6 fusion.18
  124.8 1.3 dynamic-slice
  126.8 1.3 convolution_convert_fusion
  128.1 559.2 %all-reduce.3.cloned.1.call-done = f32[576,448]{1,0:T(8,128)} async-done(((f32[576,448]{1,0:T(8,128)}), f32[576,448]{1,0:T(8,128)}) %all-reduce.3.cloned.1.call-update) | async-done | bytes 1032208
  687.3 1.4 constant_dynamic-slice_fusion
  (25 shorter events, 0.4 us)
Async XLA Ops:
  7.2 1.5 copy-start
  7.2 1.7 copy-start.6
  7.2 85.2 %reduce-scatter.4.cloned.1.call-start = ((), (), s32[]{:S(2)}) async-start(), calls=%async_computation.1 | async-start | bytes 1392640 | tf_op jit(solution)/shard_map/reduce_scatter | solution.py:59
  8.9 1.2 copy-start.1
  8.9 1.5 copy-start.2
  12.7 0.7 copy-start.5
  12.7 81.0 %copy-start.4 = (f32[512]{0:T(512)S(1)}, f32[512]{0:T(512)}, u32[]{:S(2)}) copy-start(f32[512]{0:T(512)} %param.16) | copy-start | bytes 6148
  12.7 110.4 %copy-start.3 = (bf16[512,448]{0,1:T(8,128)(2,1)S(1)}, bf16[512,448]{0,1:T(8,128)(2,1)}, u32[]{:S(2)}) copy-start(bf16[512,448]{0,1:T(8,128)(2,1)} %param.18) | copy-start | bytes 1376260
  12.7 674.6 %all-reduce.3.cloned.1.call-start = ((), (), s32[]{:S(2)}) async-start(), calls=%async_computation.2 | async-start | bytes 2359296
  124.7 2.0 copy-start.7
Sparse Core Ops, SparseCore 0:
  12.9 79.4 reduce-scatter.3
  124.9 562.3 all-reduce.2
where the time goes:
time: 696 us
  waiting for transfers between devices  638 us (92%)
  blocking collectives  27.4 us (4%)
  between operations  14.8 us (2%)
  local copies, waits for them, and re-layouts  8.4 us (1%)
    unnamed x3, waiting for transfers between devices  559 us
    reduce_scatter x1, waiting for transfers between devices, on_device(): shared = lax.psum_scatter(stacked, 'head', scatter_dimension=0, tiled=True)  78.8 us
    all_gather x1, blocking collectives, on_device(): kva_grad = lax.all_gather(own_grad, 'head', axis=0, tiled=True)  27.4 us
  transfers between devices with their start and end apart: 2, of which 2 were waited for; matrix products, arithmetic and copies ran while one was open for 0% of the time, Pallas kernels for 0%

commit v1 on v0

v1 whole, which is shorter than its diff:
```python
import functools

import jax
import jax.numpy as jnp
from jax import lax
from jax.experimental import pallas as pl
from jax.experimental.pallas import tpu as pltpu
from jax.sharding import PartitionSpec as P

LATENT = 512
ROPE = 64
KVW = LATENT + ROPE
ROWS = 32
TILES = KVW * ROWS // (16 * 128)
MESH = pl.DeviceIdType.MESH
NT = (((1,), (1,)), ((), ()))
TT = (((0,), (1,)), ((), ()))
NN = (((1,), (0,)), ((), ()))
F32 = jnp.float32
BF16 = jnp.bfloat16


class Layout:
    def __init__(self, nzh, ny, nx):
        self.nzh, self.ny, self.nx = nzh, ny, nx
        self.heads = 2 * nx
        self.groups = 2 * ny * nzh
        self.seq = ROWS * self.heads
        self.own = KVW // self.groups
        self.block = -(-nzh * self.own // 8) * 8
        self.used = 2 * ny * self.block
        self.kp = -(-self.used // 128) * 128
        self.ownp = -(-self.own // 16) * 16


def far_first(n):
    return sorted(range(1, n), key=lambda d: (-min(d, n - d), d))


def dot(a, b, dims):
    return lax.dot_general(a, b, dims, preferred_element_type=F32)


def kernel(
    lay,
    key_hbm,
    value_hbm,
    rope_hbm,
    key_lift_hbm,
    value_lift_hbm,
    latent_hbm,
    gain_hbm,
    docs_hbm,
    hidden_hbm,
    down_hbm,
    hidden_out,
    weight_out,
    key_v,
    value_v,
    rope_v,
    key_lift_v,
    value_lift_v,
    latent_v,
    gain_v,
    docs_s,
    hidden_v,
    down_v,
    load_sem,
    fold_v,
    pick_v,
    down_p,
    own_a,
    zsend,
    zrecv,
    xsend,
    xrecv,
    acc_a,
    sum_a,
    kv_row,
    kva,
    w_f32,
    csend,
    crecv,
    ysend,
    yrecv,
    acc_c,
    hi_f32,
    hi_send,
    hi_recv,
    hid_v,
    out_sem,
    zs_sem,
    zr_sem,
    xs_sem,
    xr_sem,
    gs_sem,
    gr_sem,
    fs_sem,
    fr_sem,
    cs_sem,
    cr_sem,
    ys_sem,
    yr_sem,
    hs_sem,
    hr_sem,
):
    nx, ny, nzh = lay.nx, lay.ny, lay.nzh
    half = lay.seq // 2
    g = lax.axis_index("group")
    h = lax.axis_index("head")
    core, y, zh = g % 2, (g // 2) % ny, g // (2 * ny)
    x, zl = h % nx, h // nx

    z_peer = (g, (1 - zl) * nx + x)
    core_peer = (g + 1 - 2 * core, h)
    x_peer = {d: (g, zl * nx + (x + d) % nx) for d in range(1, nx)}
    y_peer = {d: ((zh * ny + (y + d) % ny) * 2 + core, h) for d in range(1, ny)}
    h_peer = {d: ((((zh + d) % nzh) * ny + y) * 2 + core, h) for d in range(1, nzh)}
    peers = [z_peer, core_peer, *x_peer.values(), *y_peer.values(), *h_peer.values()]

    barrier = pltpu.get_barrier_semaphore()
    for peer in peers:
        pl.semaphore_signal(barrier, inc=1, device_id=peer, device_id_type=MESH)

    theirs = pl.ds(pl.multiple_of((1 - zl) * half, half), half)
    mine = pl.ds(pl.multiple_of(zl * half, half), half)
    own_rows = pl.ds(pl.multiple_of(h * ROWS, ROWS), ROWS)
    loads = []

    def load(src, dst):
        copy = pltpu.make_async_copy(src, dst, load_sem.at[len(loads)])
        copy.start()
        loads.append(copy)
        return copy

    first = [
        load(key_lift_hbm, key_lift_v),
        load(key_hbm.at[theirs, :], key_v.at[0]),
        load(value_lift_hbm, value_lift_v),
        load(value_hbm.at[theirs, :], value_v.at[0]),
        load(rope_hbm.at[theirs, :], rope_v.at[0]),
    ]
    second = [
        load(key_hbm.at[mine, :], key_v.at[1]),
        load(value_hbm.at[mine, :], value_v.at[1]),
        load(rope_hbm.at[mine, :], rope_v.at[1]),
    ]
    third = [
        load(down_hbm, down_v),
        load(latent_hbm.at[own_rows, :], latent_v),
        load(gain_hbm, gain_v),
        load(docs_hbm, docs_s),
        load(hidden_hbm, hidden_v),
    ]

    width = rope_v.shape[2]
    fold_row = lax.broadcasted_iota(jnp.int32, (width, 128), 0)
    fold_col = lax.broadcasted_iota(jnp.int32, (width, 128), 1)
    fold_v[...] = jnp.where((fold_row & 63) == (fold_col & 63), 1.0, 0.0).astype(BF16)
    low = lax.broadcasted_iota(jnp.int32, (16, 128), 1) < 64

    def partial(part):
        terms = dot(key_v[part], key_lift_v[...], NT) + dot(value_v[part], value_lift_v[...], NT)
        return terms, dot(rope_v[part], fold_v[...], NN)

    def tiles(terms, ropes, chunk):
        base = chunk * ROWS
        for block in range(2):
            rows = slice(base + 16 * block, base + 16 * block + 16)
            for lane in range(4):
                yield 4 * block + lane, terms[rows, 128 * lane : 128 * lane + 128]
        yield 8, jnp.where(low, ropes[base : base + 16], ropes[base + 16 : base + 32])

    for copy in first:
        copy.wait()
    terms, ropes = partial(0)
    for chunk in range(nx):
        for i, tile in tiles(terms, ropes, chunk):
            zsend[chunk, i] = tile.astype(BF16)
    pl.semaphore_wait(barrier, len(peers))

    order = far_first(nx) + [0]
    z_copies = {}
    for d in order:
        to = (x + d) % nx
        z_copies[d] = pltpu.make_async_remote_copy(
            zsend.at[to], zrecv.at[to], zs_sem.at[d], zr_sem.at[d], device_id=z_peer, device_id_type=MESH
        )
        z_copies[d].start()
    for copy in second:
        copy.wait()
    terms, ropes = partial(1)
    for chunk in range(nx):
        for i, tile in tiles(terms, ropes, chunk):
            own_a[chunk, i] = tile

    x_copies = {}
    for d in order:
        to = (x + d) % nx
        z_copies[d].wait_recv()
        total = own_a[to] + zrecv[to].astype(F32)
        if d == 0:
            acc_a[...] = total
        else:
            xsend[d] = total.astype(BF16)
            x_copies[d] = pltpu.make_async_remote_copy(
                xsend.at[d], xrecv.at[d], xs_sem.at[d], xr_sem.at[d], device_id=x_peer[d], device_id_type=MESH
            )
            x_copies[d].start()

    for copy in third:
        copy.wait()
    block, own = lay.block, lay.own
    col = lax.broadcasted_iota(jnp.int32, (KVW, lay.kp), 1)
    row = lax.broadcasted_iota(jnp.int32, (KVW, lay.kp), 0)
    chunk_of = jnp.zeros_like(col)
    for k in range(1, 2 * ny):
        chunk_of = chunk_of + jnp.where(col >= k * block, 1, 0)
    q = col - chunk_of * block
    hi_of = jnp.zeros_like(col)
    for k in range(1, nzh):
        hi_of = hi_of + jnp.where(q >= k * own, 1, 0)
    core_of = jnp.where(chunk_of >= ny, 1, 0)
    source = ((hi_of * ny + chunk_of - core_of * ny) * 2 + core_of) * own + q - hi_of * own
    picked = (row == source) & (q < nzh * own) & (col < lay.used)
    pick_v[...] = jnp.where(picked, 1.0, 0.0).astype(BF16)
    down_p[...] = dot(down_v[...], pick_v[...], NN).astype(BF16)

    lane = lax.broadcasted_iota(jnp.int32, (16, 128), 1)
    token = h * ROWS + lax.broadcasted_iota(jnp.int32, (16, 128), 0) + jnp.where(low, 0, 16)
    start = jnp.zeros_like(token)
    end = jnp.int32(0)
    for k in range(docs_s.shape[1]):
        end = end + docs_s[0, k]
        start = jnp.maximum(start, jnp.where(token >= end, end, 0))
    position = (token - start).astype(F32)
    pair = (lane & 31).astype(F32)
    angle = position * jnp.exp(pair * (-2.0 / ROPE * 9.210340371976184))
    cosine, sine = jnp.cos(angle), jnp.sin(angle)
    front = (lane & 32) == 0
    sine = jnp.where(front, sine, -sine)
    values = latent_v[...].astype(F32)
    inverse = lax.rsqrt(jnp.mean(values * values, axis=1, keepdims=True) + 1e-06)

    for d in far_first(nx):
        x_copies[d].wait_recv()
        acc_a[...] += xrecv[d].astype(F32)

    for rb in range(2):
        for lb in range(4):
            sum_a[16 * rb : 16 * rb + 16, 128 * lb : 128 * lb + 128] = acc_a[4 * rb + lb]
    scaled = sum_a[...] * gain_v[...]
    dots = jnp.mean(scaled * values, axis=1, keepdims=True)
    kv_row[:, :LATENT] = (inverse * (scaled - values * inverse * inverse * dots)).astype(BF16)
    rope = acc_a[8]
    other = jnp.where(front, pltpu.roll(rope, 96, 1), pltpu.roll(rope, 32, 1))
    rotated = rope * cosine + other * sine
    kv_row[0:16, LATENT:KVW] = rotated[:, :ROPE].astype(BF16)
    kv_row[16:32, LATENT:KVW] = pltpu.roll(rotated, 64, 1)[:, :ROPE].astype(BF16)
    kva[own_rows, :] = dot(kv_row[...], pick_v[...], NN).astype(BF16)

    def rows_of(head):
        return pl.ds(pl.multiple_of(head * ROWS, ROWS), ROWS)

    def gather_copy(head, send, recv, peer):
        rows = kva.at[rows_of(head), :]
        copy = pltpu.make_async_remote_copy(rows, rows, send, recv, device_id=peer, device_id_type=MESH)
        copy.start()
        return copy

    g_copies = {}
    for d in far_first(nx):
        g_copies[d] = gather_copy(h, gs_sem.at[d], gr_sem.at[d], x_peer[d])
    f_copies = {0: gather_copy(h, fs_sem.at[0], fr_sem.at[0], z_peer)}
    for d in reversed(far_first(nx)):
        g_copies[d].wait_recv()
        f_copies[d] = gather_copy(zl * nx + (x - d + nx) % nx, fs_sem.at[d], fr_sem.at[d], z_peer)
    for d in f_copies:
        f_copies[d].wait_recv()

    product = dot(kva[...], hidden_v[...], TT)
    for k in range(2):
        for j in range(ny):
            at = (k * ny + j) * block
            w_f32[k, j] = product[at : at + block].reshape(w_f32.shape[2:])
    csend[...] = w_f32[1 - core].astype(BF16)
    c_copies, y_copies = {}, {}
    order = far_first(ny) + [0]
    for d in order:
        to = (y + d) % ny
        c_copies[d] = pltpu.make_async_remote_copy(
            csend.at[to], crecv.at[to], cs_sem.at[d], cr_sem.at[d], device_id=core_peer, device_id_type=MESH
        )
        c_copies[d].start()
    total = None
    for d in order:
        to = (y + d) % ny
        c_copies[d].wait_recv()
        total = w_f32[core, to] + crecv[to].astype(F32)
        if d != 0:
            ysend[d] = total.astype(BF16)
            y_copies[d] = pltpu.make_async_remote_copy(
                ysend.at[d], yrecv.at[d], ys_sem.at[d], yr_sem.at[d], device_id=y_peer[d], device_id_type=MESH
            )
            y_copies[d].start()

    hid_v[...] = dot(down_p[...], kva[...], NT).astype(BF16)
    out_copy = pltpu.make_async_copy(hid_v, hidden_out, out_sem)
    out_copy.start()

    for d in far_first(ny):
        y_copies[d].wait_recv()
        total = total + yrecv[d].astype(F32)
    acc_c[...] = total.reshape(acc_c.shape)
    for k in range(nzh):
        piece = acc_c[k * own : k * own + own, :]
        hi_f32[k, 0:own, :] = piece
        hi_send[k, 0:own, :] = piece.astype(BF16)
    h_copies = {}
    for d in far_first(nzh):
        to = (zh + d) % nzh
        h_copies[d] = pltpu.make_async_remote_copy(
            hi_send.at[to], hi_recv.at[d], hs_sem.at[d], hr_sem.at[d], device_id=h_peer[d], device_id_type=MESH
        )
        h_copies[d].start()
    result = hi_f32[zh, 0:own, :]
    for d in far_first(nzh):
        h_copies[d].wait_recv()
        result = result + hi_recv[d, 0:own, :].astype(F32)
    weight_out[...] = result

    for copies in (z_copies, x_copies, g_copies, f_copies, c_copies, y_copies, h_copies):
        for copy in copies.values():
            copy.wait_send()
    out_copy.wait()


def on_device(lay, *args):
    key, value, rope, key_lift, value_lift, latent, gain, docs, hidden, down = args
    half = lay.seq // 2
    nx, ny, nzh = lay.nx, lay.ny, lay.nzh
    hidden = hidden.T
    cols = hidden.shape[0]
    rows8 = (lay.block // 8, 8, cols)
    dma = pltpu.SemaphoreType.DMA
    any_spec = pl.BlockSpec(memory_space=pl.ANY)
    scratch = [
        pltpu.VMEM((2, half, key.shape[1]), BF16),
        pltpu.VMEM((2, half, value.shape[1]), BF16),
        pltpu.VMEM((2, half, rope.shape[1]), BF16),
        pltpu.VMEM(key_lift.shape, BF16),
        pltpu.VMEM(value_lift.shape, BF16),
        pltpu.VMEM((ROWS, LATENT), BF16),
        pltpu.VMEM((1, LATENT), F32),
        pltpu.SMEM(docs.shape, jnp.int32),
        pltpu.VMEM(hidden.shape, BF16),
        pltpu.VMEM(down.shape, BF16),
        dma((13,)),
        pltpu.VMEM((rope.shape[1], 128), BF16),
        pltpu.VMEM((KVW, lay.kp), BF16),
        pltpu.VMEM((down.shape[0], lay.kp), BF16),
        pltpu.VMEM((nx, TILES, 16, 128), F32),
        pltpu.VMEM((nx, TILES, 16, 128), BF16),
        pltpu.VMEM((nx, TILES, 16, 128), BF16),
        pltpu.VMEM((nx, TILES, 16, 128), BF16),
        pltpu.VMEM((nx, TILES, 16, 128), BF16),
        pltpu.VMEM((TILES, 16, 128), F32),
        pltpu.VMEM((ROWS, LATENT), F32),
        pltpu.VMEM((ROWS, KVW), BF16),
        pltpu.VMEM((lay.seq, lay.kp), BF16),
        pltpu.VMEM((2, ny, *rows8), F32),
        pltpu.VMEM((ny, *rows8), BF16),
        pltpu.VMEM((ny, *rows8), BF16),
        pltpu.VMEM((ny, *rows8), BF16),
        pltpu.VMEM((ny, *rows8), BF16),
        pltpu.VMEM((lay.block, cols), F32),
        pltpu.VMEM((nzh, lay.ownp, cols), F32),
        pltpu.VMEM((nzh, lay.ownp, cols), BF16),
        pltpu.VMEM((nzh, lay.ownp, cols), BF16),
        pltpu.VMEM((cols, lay.seq), BF16),
        dma,
        *[dma((nx,))] * 8,
        *[dma((ny,))] * 4,
        *[dma((nzh,))] * 2,
    ]
    hidden_grad, weight_grad = pl.pallas_call(
        functools.partial(kernel, lay),
        out_shape=(
            jax.ShapeDtypeStruct((cols, lay.seq), BF16),
            jax.ShapeDtypeStruct((lay.own, cols), F32),
        ),
        in_specs=[any_spec] * 10,
        out_specs=(any_spec, pl.BlockSpec(memory_space=pltpu.VMEM)),
        scratch_shapes=scratch,
        compiler_params=pltpu.CompilerParams(
            collective_id=0, has_side_effects=True, vmem_limit_bytes=60 * 1024 * 1024
        ),
        name="latent_backward",
    )(key, value, rope, key_lift, value_lift, latent, gain.reshape(1, -1), docs, hidden, down)
    return hidden_grad.T, weight_grad


def solution(mesh, lay=Layout(4, 8, 8)):
    return jax.shard_map(
        functools.partial(on_device, lay),
        mesh=mesh,
        in_specs=(
            P("group", "head"),
            P("group", "head"),
            P("group", "head"),
            P(None, "head"),
            P(None, "head"),
            P("group", None),
            P(),
            P("group", None),
            P("group", "head"),
            P("head", None),
        ),
        out_specs=(P("group", "head"), P("group", "head")),
        check_vma=False,
    )
```

time: 696 us -> 68.3 us (0.10)
  waiting for transfers between devices: 638 us -> 0 us
  Pallas kernels: 0 us -> 65 us
  blocking collectives: 27.4 us -> 0 us
  between operations: 14.8 us -> 0.65 us
    unnamed x3 -> x0, waiting for transfers between devices: 559 us -> none
    reduce_scatter x1 -> x0, waiting for transfers between devices: 78.8 us -> none  [on_device(): shared = lax.psum_scatter(stacked, 'head', scatter_dimension=0, tiled=True)]
    pallas_call x0 -> x1, Pallas kernels: none -> 65 us  [on_device(): pl.pallas_call(functools.partial(kernel, lay), out_shape=(jax.ShapeDtypeS...]
    all_gather x1 -> x0, blocking collectives: 27.4 us -> none  [on_device(): kva_grad = lax.all_gather(own_grad, 'head', axis=0, tiled=True)]
  transfers between devices with their start and end apart: 2 -> 0, of which waited for: 2 -> 0; matrix products, arithmetic and copies ran while one was open for 0% -> 0% of each run, Pallas kernels for 0% -> 0%
where the time goes in v1:
time: 68.3 us; the launch traced here: 68.1 us
  Pallas kernels  65 us (95%)
  local copies, waits for them, and re-layouts  2.44 us (4%)
    pallas_call x1, Pallas kernels, on_device(): pl.pallas_call(functools.partial(kernel, lay), out_shape=(jax.ShapeDtypeS...  65 us
    unnamed x4, local copies, waits for them, and re-layouts  2.44 us

profile of v1, /device:TPU:1, one launch (start us, length us, event | category | flops | bytes accessed | tf_op | source)
XLA Modules:
  0.0 68.1 jit_solution(2566000133256614405)
XLA Ops:
  0.6 65.0 %latent_backward.1 = (bf16[448,512]{1,0:T(8,128)(2,1)}, f32[9,448]{1,0:T(8,128)}) custom-call(bf16[512,1024]{1,0:T(8,128)(2,1)} %key_hbm.1, bf16[512,1024]{1,0:T(8,128)(2,1)} %value_hbm.1, bf16[512,512]{1,0:T(8,128)(2,1)} %rope_hbm.1, bf16[512,1024]{1,0:T(8,128)(2,1)} %key_lift_hbm.1, bf16[512,1024]{1,0:T(8,128)(2,1)} %value_lift_hbm.1, ...), custom_call_target="tpu_custom_call" | custom-call | tf_op jit(solution)/shard_map/latent_backward/pallas_call | solution.py:386
  65.6 0.0 copy-start
  65.7 1.8 %copy.14 = bf16[512,448]{0,1:T(8,128)(2,1)} copy(bf16[512,448]{0,1:T(8,128)(2,1)} %bitcast.4) | data formatting | bytes 917504
  67.5 0.0 copy-done
  67.5 0.6 copy.15
Async XLA Ops:
  65.6 1.8 %copy-start = (f32[9,448]{1,0:T(8,128)S(1)}, f32[9,448]{1,0:T(8,128)}, u32[]{:S(2)}) copy-start(f32[9,448]{1,0:T(8,128)} %get-tuple-element.9) | copy-start | bytes 48388

commit v2 on v1

--- a/solution.py
+++ b/solution.py
@@ -35,6 +35,81 @@
 
 def far_first(n):
     return sorted(range(1, n), key=lambda d: (-min(d, n - d), d))
+
+
+def remote(src, dst, send, recv, peer):
+    return pltpu.make_async_remote_copy(src, dst, send, recv, device_id=peer, device_id_type=MESH)
+
+
+class Ring:
+    PLAN = {"far": (0, 3, 1), "raf": (1, -3, -1), "add": (3, 2, 2), "dda": (4, -2, -2), "one": (5, 1, 1), "eno": (6, -1, -1)}
+
+    def __init__(self, peer, send, recv, send_sem, recv_sem, split):
+        self.peer, self.send, self.recv, self.split = peer, send, recv, split
+        self.send_sem, self.recv_sem = send_sem, recv_sem
+        self.copies = {}
+
+    def start(self, name, src, dst, sem, hop):
+        self.copies[name] = remote(src, dst, self.send_sem, self.recv_sem.at[sem], self.peer[hop])
+        self.copies[name].start()
+
+    def put(self, name, term):
+        slot, _, hop = self.PLAN[name]
+        self.send[slot] = term.astype(BF16)
+        self.start(name, self.send.at[slot], self.recv.at[slot], slot, hop)
+
+    def put_opposite(self, term):
+        self.send[2] = term.astype(BF16)
+        first, second = pl.ds(0, self.split), pl.ds(self.split, self.send.shape[1] - self.split)
+        self.start("first", self.send.at[2, first], self.recv.at[2, first], 2, 2)
+        self.start("second", self.send.at[2, second], self.recv.at[2, second], 7, -2)
+
+    def take(self, name):
+        self.copies[name].wait_recv()
+        return self.recv[self.PLAN[name][0]].astype(F32)
+
+    def relay(self, name, term_ref, index):
+        far, part = ("far", "first") if name == "add" else ("raf", "second")
+        self.copies[far].wait_recv()
+        self.copies[part].wait_recv()
+        rows = pl.ds(0, self.split) if name == "add" else pl.ds(self.split, self.send.shape[1] - self.split)
+        slot = self.PLAN[far][0]
+        term_ref[index] = term_ref[index] + self.recv[slot].astype(F32)
+        whole = term_ref.at[index]
+        whole[rows] = whole[rows] + self.recv[2, rows].astype(F32)
+        self.put(name, term_ref[index])
+
+    def reduce(self, size, me, ready, term_ref):
+        def at(offset):
+            return (me + offset + size) % size
+
+        def term(offset):
+            ready(offset % size, at(offset))
+            return term_ref[at(offset)]
+
+        if size == 1:
+            return term(0)
+        self.put_opposite(term(4))
+        self.put("far", term(3))
+        self.put("raf", term(-3))
+        ready(2, at(2))
+        ready(6, at(-2))
+        self.relay("add", term_ref, at(2))
+        self.relay("dda", term_ref, at(-2))
+        self.put("one", term(1))
+        self.put("eno", term(-1))
+        return term(0)
+
+    def collect(self, size, total):
+        if size == 1:
+            return total
+        for name in ("one", "eno", "add", "dda"):
+            total = total + self.take(name)
+        return total
+
+    def finish(self, size):
+        if size > 1:
+            remote(self.send, self.recv, self.send_sem, self.recv_sem.at[0], self.peer[1]).wait_send()
 
 
 def dot(a, b, dims):
@@ -87,8 +162,6 @@
     hi_f32,
     hi_send,
     hi_recv,
-    hid_v,
-    out_sem,
     zs_sem,
     zr_sem,
     xs_sem,
@@ -113,14 +186,11 @@
 
     z_peer = (g, (1 - zl) * nx + x)
     core_peer = (g + 1 - 2 * core, h)
-    x_peer = {d: (g, zl * nx + (x + d) % nx) for d in range(1, nx)}
-    y_peer = {d: ((zh * ny + (y + d) % ny) * 2 + core, h) for d in range(1, ny)}
+    near = (2, -2, 1, -1)
+    x_peer = {d: (g, zl * nx + (x + d + nx) % nx) for d in near if nx > 1}
+    y_peer = {d: ((zh * ny + (y + d + ny) % ny) * 2 + core, h) for d in near if ny > 1}
     h_peer = {d: ((((zh + d) % nzh) * ny + y) * 2 + core, h) for d in range(1, nzh)}
     peers = [z_peer, core_peer, *x_peer.values(), *y_peer.values(), *h_peer.values()]
-
-    barrier = pltpu.get_barrier_semaphore()
-    for peer in peers:
-        pl.semaphore_signal(barrier, inc=1, device_id=peer, device_id_type=MESH)
 
     theirs = pl.ds(pl.multiple_of((1 - zl) * half, half), half)
     mine = pl.ds(pl.multiple_of(zl * half, half), half)
@@ -153,6 +223,10 @@
         load(hidden_hbm, hidden_v),
     ]
 
+    barrier = pltpu.get_barrier_semaphore()
+    for peer in peers:
+        pl.semaphore_signal(barrier, inc=1, device_id=peer, device_id_type=MESH)
+
     width = rope_v.shape[2]
     fold_row = lax.broadcasted_iota(jnp.int32, (width, 128), 0)
     fold_col = lax.broadcasted_iota(jnp.int32, (width, 128), 1)
@@ -179,13 +253,11 @@
             zsend[chunk, i] = tile.astype(BF16)
     pl.semaphore_wait(barrier, len(peers))
 
-    order = far_first(nx) + [0]
+    order = [0] if nx == 1 else [4, 3, 5, 2, 6, 1, 7, 0]
     z_copies = {}
     for d in order:
         to = (x + d) % nx
-        z_copies[d] = pltpu.make_async_remote_copy(
-            zsend.at[to], zrecv.at[to], zs_sem.at[d], zr_sem.at[d], device_id=z_peer, device_id_type=MESH
-        )
+        z_copies[d] = remote(zsend.at[to], zrecv.at[to], zs_sem, zr_sem.at[d], z_peer)
         z_copies[d].start()
     for copy in second:
         copy.wait()
@@ -193,20 +265,6 @@
     for chunk in range(nx):
         for i, tile in tiles(terms, ropes, chunk):
             own_a[chunk, i] = tile
-
-    x_copies = {}
-    for d in order:
-        to = (x + d) % nx
-        z_copies[d].wait_recv()
-        total = own_a[to] + zrecv[to].astype(F32)
-        if d == 0:
-            acc_a[...] = total
-        else:
-            xsend[d] = total.astype(BF16)
-            x_copies[d] = pltpu.make_async_remote_copy(
-                xsend.at[d], xrecv.at[d], xs_sem.at[d], xr_sem.at[d], device_id=x_peer[d], device_id_type=MESH
-            )
-            x_copies[d].start()
 
     for copy in third:
         copy.wait()
@@ -242,9 +300,13 @@
     values = latent_v[...].astype(F32)
     inverse = lax.rsqrt(jnp.mean(values * values, axis=1, keepdims=True) + 1e-06)
 
-    for d in far_first(nx):
-        x_copies[d].wait_recv()
-        acc_a[...] += xrecv[d].astype(F32)
+    def from_z(offset, owner):
+        z_copies[offset].wait_recv()
+        own_a[owner] = own_a[owner] + zrecv[owner].astype(F32)
+
+    x_ring = Ring(x_peer, xsend, xrecv, xs_sem, xr_sem, 5)
+    mine_a = x_ring.reduce(nx, x, from_z, own_a)
+    acc_a[...] = x_ring.collect(nx, mine_a)
 
     for rb in range(2):
         for lb in range(4):
@@ -259,24 +321,48 @@
     kv_row[16:32, LATENT:KVW] = pltpu.roll(rotated, 64, 1)[:, :ROPE].astype(BF16)
     kva[own_rows, :] = dot(kv_row[...], pick_v[...], NN).astype(BF16)
 
-    def rows_of(head):
-        return pl.ds(pl.multiple_of(head * ROWS, ROWS), ROWS)
-
-    def gather_copy(head, send, recv, peer):
-        rows = kva.at[rows_of(head), :]
-        copy = pltpu.make_async_remote_copy(rows, rows, send, recv, device_id=peer, device_id_type=MESH)
-        copy.start()
-        return copy
-
-    g_copies = {}
-    for d in far_first(nx):
-        g_copies[d] = gather_copy(h, gs_sem.at[d], gr_sem.at[d], x_peer[d])
-    f_copies = {0: gather_copy(h, fs_sem.at[0], fr_sem.at[0], z_peer)}
-    for d in reversed(far_first(nx)):
-        g_copies[d].wait_recv()
-        f_copies[d] = gather_copy(zl * nx + (x - d + nx) % nx, fs_sem.at[d], fr_sem.at[d], z_peer)
-    for d in f_copies:
-        f_copies[d].wait_recv()
+    def block_at(offset, part=None):
+        head = zl * nx + (x + offset + nx) % nx
+        first, size = (0, ROWS) if part is None else (part * ROWS // 2, ROWS // 2)
+        return kva.at[pl.ds(pl.multiple_of(head * ROWS + first, size), size), :]
+
+    g_copies, f_copies = {}, {}
+
+    def along(name, rows, sem, hop):
+        g_copies[name] = remote(rows, rows, gs_sem, gr_sem.at[sem], x_peer[hop])
+        g_copies[name].start()
+
+    def across(rows):
+        sem = len(f_copies)
+        f_copies[sem] = remote(rows, rows, fs_sem, fr_sem.at[sem], z_peer)
+        f_copies[sem].start()
+
+    if nx > 1:
+        for sem, hop in enumerate(near):
+            along(hop, block_at(0), sem, hop)
+    across(block_at(0))
+    if nx > 1:
+        g_copies[2].wait_recv()
+        along("far", block_at(-2), 4, 1)
+        along("first", block_at(-2, 0), 5, 2)
+        g_copies[-2].wait_recv()
+        along("raf", block_at(2), 6, -1)
+        along("second", block_at(2, 1), 7, -2)
+        for hop in (1, -1):
+            g_copies[hop].wait_recv()
+            across(block_at(-hop))
+        across(block_at(-2))
+        across(block_at(2))
+        g_copies["far"].wait_recv()
+        across(block_at(-3))
+        g_copies["raf"].wait_recv()
+        across(block_at(3))
+        g_copies["first"].wait_recv()
+        across(block_at(4, 0))
+        g_copies["second"].wait_recv()
+        across(block_at(4, 1))
+    for copy in f_copies.values():
+        copy.wait_recv()
 
     product = dot(kva[...], hidden_v[...], TT)
     for k in range(2):
@@ -284,33 +370,23 @@
             at = (k * ny + j) * block
             w_f32[k, j] = product[at : at + block].reshape(w_f32.shape[2:])
     csend[...] = w_f32[1 - core].astype(BF16)
-    c_copies, y_copies = {}, {}
-    order = far_first(ny) + [0]
+    c_copies = {}
+    order = [0] if ny == 1 else [4, 3, 5, 2, 6, 1, 7, 0]
     for d in order:
         to = (y + d) % ny
-        c_copies[d] = pltpu.make_async_remote_copy(
-            csend.at[to], crecv.at[to], cs_sem.at[d], cr_sem.at[d], device_id=core_peer, device_id_type=MESH
-        )
+        c_copies[d] = remote(csend.at[to], crecv.at[to], cs_sem, cr_sem.at[d], core_peer)
         c_copies[d].start()
-    total = None
-    for d in order:
-        to = (y + d) % ny
-        c_copies[d].wait_recv()
-        total = w_f32[core, to] + crecv[to].astype(F32)
-        if d != 0:
-            ysend[d] = total.astype(BF16)
-            y_copies[d] = pltpu.make_async_remote_copy(
-                ysend.at[d], yrecv.at[d], ys_sem.at[d], yr_sem.at[d], device_id=y_peer[d], device_id_type=MESH
-            )
-            y_copies[d].start()
-
-    hid_v[...] = dot(down_p[...], kva[...], NT).astype(BF16)
-    out_copy = pltpu.make_async_copy(hid_v, hidden_out, out_sem)
-    out_copy.start()
-
-    for d in far_first(ny):
-        y_copies[d].wait_recv()
-        total = total + yrecv[d].astype(F32)
+
+    own_c = w_f32.at[core]
+
+    def from_core(offset, owner):
+        c_copies[offset].wait_recv()
+        own_c[owner] = own_c[owner] + crecv[owner].astype(F32)
+
+    y_ring = Ring(y_peer, ysend, yrecv, ys_sem, yr_sem, (block // 8 + 1) // 2)
+    mine_c = y_ring.reduce(ny, y, from_core, own_c)
+    hidden_out[...] = dot(down_p[...], kva[...], NT).astype(BF16)
+    total = y_ring.collect(ny, mine_c)
     acc_c[...] = total.reshape(acc_c.shape)
     for k in range(nzh):
         piece = acc_c[k * own : k * own + own, :]
@@ -319,9 +395,7 @@
     h_copies = {}
     for d in far_first(nzh):
         to = (zh + d) % nzh
-        h_copies[d] = pltpu.make_async_remote_copy(
-            hi_send.at[to], hi_recv.at[d], hs_sem.at[d], hr_sem.at[d], device_id=h_peer[d], device_id_type=MESH
-        )
+        h_copies[d] = remote(hi_send.at[to], hi_recv.at[d], hs_sem, hr_sem.at[d], h_peer[d])
         h_copies[d].start()
     result = hi_f32[zh, 0:own, :]
     for d in far_first(nzh):
@@ -329,10 +403,18 @@
         result = result + hi_recv[d, 0:own, :].astype(F32)
     weight_out[...] = result
 
-    for copies in (z_copies, x_copies, g_copies, f_copies, c_copies, y_copies, h_copies):
-        for copy in copies.values():
-            copy.wait_send()
-    out_copy.wait()
+    remote(zsend, zrecv, zs_sem, zr_sem.at[0], z_peer).wait_send()
+    x_ring.finish(nx)
+    if nx > 1:
+        sent = kva.at[pl.ds(0, 7 * ROWS), :]
+        remote(sent, sent, gs_sem, gr_sem.at[0], x_peer[1]).wait_send()
+    passed = kva.at[pl.ds(0, nx * ROWS), :]
+    remote(passed, passed, fs_sem, fr_sem.at[0], z_peer).wait_send()
+    remote(csend, crecv, cs_sem, cr_sem.at[0], core_peer).wait_send()
+    y_ring.finish(ny)
+    if nzh > 1:
+        sent = pl.ds(1, nzh - 1)
+        remote(hi_send.at[sent], hi_recv.at[sent], hs_sem, hr_sem.at[1], core_peer).wait_send()
 
 
 def on_device(lay, *args):
@@ -362,8 +444,8 @@
         pltpu.VMEM((nx, TILES, 16, 128), F32),
         pltpu.VMEM((nx, TILES, 16, 128), BF16),
         pltpu.VMEM((nx, TILES, 16, 128), BF16),
-        pltpu.VMEM((nx, TILES, 16, 128), BF16),
-        pltpu.VMEM((nx, TILES, 16, 128), BF16),
+        pltpu.VMEM((7, TILES, 16, 128), BF16),
+        pltpu.VMEM((7, TILES, 16, 128), BF16),
         pltpu.VMEM((TILES, 16, 128), F32),
         pltpu.VMEM((ROWS, LATENT), F32),
         pltpu.VMEM((ROWS, KVW), BF16),
@@ -371,26 +453,35 @@
         pltpu.VMEM((2, ny, *rows8), F32),
         pltpu.VMEM((ny, *rows8), BF16),
         pltpu.VMEM((ny, *rows8), BF16),
-        pltpu.VMEM((ny, *rows8), BF16),
-        pltpu.VMEM((ny, *rows8), BF16),
+        pltpu.VMEM((7, *rows8), BF16),
+        pltpu.VMEM((7, *rows8), BF16),
         pltpu.VMEM((lay.block, cols), F32),
         pltpu.VMEM((nzh, lay.ownp, cols), F32),
         pltpu.VMEM((nzh, lay.ownp, cols), BF16),
         pltpu.VMEM((nzh, lay.ownp, cols), BF16),
-        pltpu.VMEM((cols, lay.seq), BF16),
-        dma,
-        *[dma((nx,))] * 8,
-        *[dma((ny,))] * 4,
-        *[dma((nzh,))] * 2,
+        dma,
+        dma((8,)),
+        dma,
+        dma((8,)),
+        dma,
+        dma((8,)),
+        dma,
+        dma((9,)),
+        dma,
+        dma((8,)),
+        dma,
+        dma((8,)),
+        dma,
+        dma((nzh,)),
     ]
     hidden_grad, weight_grad = pl.pallas_call(
         functools.partial(kernel, lay),
         out_shape=(
-            jax.ShapeDtypeStruct((cols, lay.seq), BF16),
-            jax.ShapeDtypeStruct((lay.own, cols), F32),
+            pltpu.VMEM((cols, lay.seq), BF16),
+            pltpu.VMEM((lay.own, cols), F32),
         ),
         in_specs=[any_spec] * 10,
-        out_specs=(any_spec, pl.BlockSpec(memory_space=pltpu.VMEM)),
+        out_specs=(pl.BlockSpec(memory_space=pltpu.VMEM),) * 2,
         scratch_shapes=scratch,
         compiler_params=pltpu.CompilerParams(
             collective_id=0, has_side_effects=True, vmem_limit_bytes=60 * 1024 * 1024

time: 68.3 us -> 62.8 us (0.919)
  Pallas kernels: 65 us -> 60.6 us
  local copies, waits for them, and re-layouts: 2.44 us -> 1.38 us
    pallas_call x1, Pallas kernels: 65 us -> 60.6 us  [on_device(): pl.pallas_call(functools.partial(kernel, lay), out_shape=(pltpu.VMEM((col...]
    unnamed x4 -> x2, local copies, waits for them, and re-layouts: 2.44 us -> 1.38 us
where the time goes in v2:
time: 62.8 us; the launch traced here: 62.6 us
  Pallas kernels  60.6 us (96%)
  local copies, waits for them, and re-layouts  1.38 us (2%)
  between operations  0.64 us (1%)
    pallas_call x1, Pallas kernels, on_device(): pl.pallas_call(functools.partial(kernel, lay), out_shape=(pltpu.VMEM((col...  60.6 us
    unnamed x2, local copies, waits for them, and re-layouts  1.38 us

profile of v2, /device:TPU:1, one launch (start us, length us, event | category | flops | bytes accessed | tf_op | source)
XLA Modules:
  0.0 62.6 jit_solution(11211443553209133069)
XLA Ops:
  0.6 60.6 %latent_backward.1 = (bf16[448,512]{1,0:T(8,128)(2,1)S(1)}, f32[9,448]{1,0:T(8,128)S(1)}) custom-call(bf16[512,1024]{1,0:T(8,128)(2,1)} %key_hbm.1, bf16[512,1024]{1,0:T(8,128)(2,1)} %value_hbm.1, bf16[512,512]{1,0:T(8,128)(2,1)} %rope_hbm.1, bf16[512,1024]{1,0:T(8,128)(2,1)} %key_lift_hbm.1, bf16[512,1024]{1,0:T(8,128)(2,1)} %value_lift_hbm.1, ...), custom_call_target="tpu_custom_call" | custom-call | tf_op jit(solution)/shard_map/latent_backward/pallas_call | solution.py:477
  61.2 0.8 %copy.14 = bf16[512,448]{0,1:T(8,128)(2,1)} copy(bf16[512,448]{0,1:T(8,128)(2,1)S(1)} %bitcast.3) | data formatting | bytes 917504
  62.0 0.6 copy.15

commit v3 on v2

--- a/solution.py
+++ b/solution.py
@@ -44,8 +44,9 @@
 class Ring:
     PLAN = {"far": (0, 3, 1), "raf": (1, -3, -1), "add": (3, 2, 2), "dda": (4, -2, -2), "one": (5, 1, 1), "eno": (6, -1, -1)}
 
-    def __init__(self, peer, send, recv, send_sem, recv_sem, split):
+    def __init__(self, peer, send, recv, send_sem, recv_sem, split, direct=False):
         self.peer, self.send, self.recv, self.split = peer, send, recv, split
+        self.direct = direct
         self.send_sem, self.recv_sem = send_sem, recv_sem
         self.copies = {}
 
@@ -54,7 +55,8 @@
         self.copies[name].start()
 
     def put(self, name, term):
-        slot, _, hop = self.PLAN[name]
+        slot, offset, hop = self.PLAN[name]
+        hop = offset if self.direct else hop
         self.send[slot] = term.astype(BF16)
         self.start(name, self.send.at[slot], self.recv.at[slot], slot, hop)
 
@@ -70,16 +72,17 @@
 
     def relay(self, name, term_ref, index):
         far, part = ("far", "first") if name == "add" else ("raf", "second")
-        self.copies[far].wait_recv()
+        if not self.direct:
+            self.copies[far].wait_recv()
         self.copies[part].wait_recv()
         rows = pl.ds(0, self.split) if name == "add" else pl.ds(self.split, self.send.shape[1] - self.split)
-        slot = self.PLAN[far][0]
-        term_ref[index] = term_ref[index] + self.recv[slot].astype(F32)
+        if not self.direct:
+            term_ref[index] = term_ref[index] + self.recv[self.PLAN[far][0]].astype(F32)
         whole = term_ref.at[index]
         whole[rows] = whole[rows] + self.recv[2, rows].astype(F32)
         self.put(name, term_ref[index])
 
-    def reduce(self, size, me, ready, term_ref):
+    def reduce(self, size, me, ready, term_ref, near_first):
         def at(offset):
             return (me + offset + size) % size
 
@@ -89,21 +92,25 @@
 
         if size == 1:
             return term(0)
+        if near_first:
+            self.put("one", term(1))
+            self.put("eno", term(-1))
         self.put_opposite(term(4))
         self.put("far", term(3))
         self.put("raf", term(-3))
+        if not near_first:
+            self.put("one", term(1))
+            self.put("eno", term(-1))
         ready(2, at(2))
         ready(6, at(-2))
         self.relay("add", term_ref, at(2))
         self.relay("dda", term_ref, at(-2))
-        self.put("one", term(1))
-        self.put("eno", term(-1))
         return term(0)
 
     def collect(self, size, total):
         if size == 1:
             return total
-        for name in ("one", "eno", "add", "dda"):
+        for name in ("one", "eno", *(("far", "raf") if self.direct else ()), "add", "dda"):
             total = total + self.take(name)
         return total
 
@@ -147,6 +154,8 @@
     own_a,
     zsend,
     zrecv,
+    precv,
+    zsum,
     xsend,
     xrecv,
     acc_a,
@@ -164,6 +173,8 @@
     hi_recv,
     zs_sem,
     zr_sem,
+    ps_sem,
+    pr_sem,
     xs_sem,
     xr_sem,
     gs_sem,
@@ -187,7 +198,7 @@
     z_peer = (g, (1 - zl) * nx + x)
     core_peer = (g + 1 - 2 * core, h)
     near = (2, -2, 1, -1)
-    x_peer = {d: (g, zl * nx + (x + d + nx) % nx) for d in near if nx > 1}
+    x_peer = {d: (g, zl * nx + (x + d + nx) % nx) for d in (3, -3, *near) if nx > 1}
     y_peer = {d: ((zh * ny + (y + d + ny) % ny) * 2 + core, h) for d in near if ny > 1}
     h_peer = {d: ((((zh + d) % nzh) * ny + y) * 2 + core, h) for d in range(1, nzh)}
     peers = [z_peer, core_peer, *x_peer.values(), *y_peer.values(), *h_peer.values()]
@@ -203,24 +214,11 @@
         loads.append(copy)
         return copy
 
-    first = [
-        load(key_lift_hbm, key_lift_v),
-        load(key_hbm.at[theirs, :], key_v.at[0]),
+    first = [load(key_lift_hbm, key_lift_v), load(key_hbm.at[theirs, :], key_v.at[0])]
+    second = [
         load(value_lift_hbm, value_lift_v),
         load(value_hbm.at[theirs, :], value_v.at[0]),
         load(rope_hbm.at[theirs, :], rope_v.at[0]),
-    ]
-    second = [
-        load(key_hbm.at[mine, :], key_v.at[1]),
-        load(value_hbm.at[mine, :], value_v.at[1]),
-        load(rope_hbm.at[mine, :], rope_v.at[1]),
-    ]
-    third = [
-        load(down_hbm, down_v),
-        load(latent_hbm.at[own_rows, :], latent_v),
-        load(gain_hbm, gain_v),
-        load(docs_hbm, docs_s),
-        load(hidden_hbm, hidden_v),
     ]
 
     barrier = pltpu.get_barrier_semaphore()
@@ -232,10 +230,6 @@
     fold_col = lax.broadcasted_iota(jnp.int32, (width, 128), 1)
     fold_v[...] = jnp.where((fold_row & 63) == (fold_col & 63), 1.0, 0.0).astype(BF16)
     low = lax.broadcasted_iota(jnp.int32, (16, 128), 1) < 64
-
-    def partial(part):
-        terms = dot(key_v[part], key_lift_v[...], NT) + dot(value_v[part], value_lift_v[...], NT)
-        return terms, dot(rope_v[part], fold_v[...], NN)
 
     def tiles(terms, ropes, chunk):
         base = chunk * ROWS
@@ -247,26 +241,48 @@
 
     for copy in first:
         copy.wait()
-    terms, ropes = partial(0)
+    terms = dot(key_v[0], key_lift_v[...], NT)
+    for copy in second:
+        copy.wait()
+    third = [
+        load(key_hbm.at[mine, :], key_v.at[1]),
+        load(value_hbm.at[mine, :], value_v.at[1]),
+        load(rope_hbm.at[mine, :], rope_v.at[1]),
+    ]
+    fourth = [
+        load(down_hbm, down_v),
+        load(latent_hbm.at[own_rows, :], latent_v),
+        load(gain_hbm, gain_v),
+        load(docs_hbm, docs_s),
+        load(hidden_hbm, hidden_v),
+    ]
+    terms = terms + dot(value_v[0], value_lift_v[...], NT)
+    ropes = dot(rope_v[0], fold_v[...], NN)
     for chunk in range(nx):
         for i, tile in tiles(terms, ropes, chunk):
             zsend[chunk, i] = tile.astype(BF16)
     pl.semaphore_wait(barrier, len(peers))
 
-    order = [0] if nx == 1 else [4, 3, 5, 2, 6, 1, 7, 0]
-    z_copies = {}
+    order = [0] if nx == 1 else [4, 3, 5, 2, 6]
+    z_copies, p_copies = {}, {}
     for d in order:
         to = (x + d) % nx
         z_copies[d] = remote(zsend.at[to], zrecv.at[to], zs_sem, zr_sem.at[d], z_peer)
         z_copies[d].start()
-    for copy in second:
+        if d == 4:
+            for slot, hop in enumerate((1, -1)):
+                to = (x + hop + nx) % nx
+                p_copies[slot] = remote(zsend.at[to], precv.at[slot], ps_sem, pr_sem.at[slot], x_peer[hop])
+                p_copies[slot].start()
+    for copy in third:
         copy.wait()
-    terms, ropes = partial(1)
+    terms = dot(key_v[1], key_lift_v[...], NT) + dot(value_v[1], value_lift_v[...], NT)
+    ropes = dot(rope_v[1], fold_v[...], NN)
     for chunk in range(nx):
         for i, tile in tiles(terms, ropes, chunk):
             own_a[chunk, i] = tile
 
-    for copy in third:
+    for copy in fourth:
         copy.wait()
     block, own = lay.block, lay.own
     col = lax.broadcasted_iota(jnp.int32, (KVW, lay.kp), 1)
@@ -301,11 +317,21 @@
     inverse = lax.rsqrt(jnp.mean(values * values, axis=1, keepdims=True) + 1e-06)
 
     def from_z(offset, owner):
+        if offset in (1, 7):
+            return
+        if offset == 3:
+            near_sum = zsend[x].astype(F32)
+            for slot in p_copies:
+                p_copies[slot].wait_recv()
+                near_sum = near_sum + precv[slot].astype(F32)
+            zsum[...] = near_sum.astype(BF16)
+            z_copies[0] = remote(zsum, zrecv.at[x], zs_sem, zr_sem.at[0], z_peer)
+            z_copies[0].start()
         z_copies[offset].wait_recv()
         own_a[owner] = own_a[owner] + zrecv[owner].astype(F32)
 
-    x_ring = Ring(x_peer, xsend, xrecv, xs_sem, xr_sem, 5)
-    mine_a = x_ring.reduce(nx, x, from_z, own_a)
+    x_ring = Ring(x_peer, xsend, xrecv, xs_sem, xr_sem, 5, direct=True)
+    mine_a = x_ring.reduce(nx, x, from_z, own_a, True)
     acc_a[...] = x_ring.collect(nx, mine_a)
 
     for rb in range(2):
@@ -321,48 +347,53 @@
     kv_row[16:32, LATENT:KVW] = pltpu.roll(rotated, 64, 1)[:, :ROPE].astype(BF16)
     kva[own_rows, :] = dot(kv_row[...], pick_v[...], NN).astype(BF16)
 
-    def block_at(offset, part=None):
-        head = zl * nx + (x + offset + nx) % nx
+    def block_at(offset, part=None, plane=None):
+        head = (zl if plane is None else plane) * nx + (x + offset + nx) % nx
         first, size = (0, ROWS) if part is None else (part * ROWS // 2, ROWS // 2)
         return kva.at[pl.ds(pl.multiple_of(head * ROWS + first, size), size), :]
 
     g_copies, f_copies = {}, {}
 
-    def along(name, rows, sem, hop):
-        g_copies[name] = remote(rows, rows, gs_sem, gr_sem.at[sem], x_peer[hop])
+    def along(name, rows, hop):
+        g_copies[name] = remote(rows, rows, gs_sem, gr_sem.at[len(g_copies)], x_peer[hop])
         g_copies[name].start()
 
-    def across(rows):
-        sem = len(f_copies)
-        f_copies[sem] = remote(rows, rows, fs_sem, fr_sem.at[sem], z_peer)
-        f_copies[sem].start()
+    def across(name, rows):
+        f_copies[name] = remote(rows, rows, fs_sem, fr_sem.at[len(f_copies)], z_peer)
+        f_copies[name].start()
 
     if nx > 1:
-        for sem, hop in enumerate(near):
-            along(hop, block_at(0), sem, hop)
-    across(block_at(0))
+        along(2, block_at(0), 2)
+        along(-2, block_at(0), -2)
+    across(0, block_at(0))
     if nx > 1:
+        along(1, block_at(0), 1)
+        along(-1, block_at(0), -1)
+        f_copies[0].wait_recv()
+        along("near", block_at(0, plane=1 - zl), 1)
+        along("raen", block_at(0, plane=1 - zl), -1)
         g_copies[2].wait_recv()
-        along("far", block_at(-2), 4, 1)
-        along("first", block_at(-2, 0), 5, 2)
+        across(-2, block_at(-2))
+        along("far", block_at(-2), 1)
+        along("first", block_at(-2, 0), 2)
         g_copies[-2].wait_recv()
-        along("raf", block_at(2), 6, -1)
-        along("second", block_at(2, 1), 7, -2)
-        for hop in (1, -1):
-            g_copies[hop].wait_recv()
-            across(block_at(-hop))
-        across(block_at(-2))
-        across(block_at(2))
-        g_copies["far"].wait_recv()
-        across(block_at(-3))
-        g_copies["raf"].wait_recv()
-        across(block_at(3))
+        across(2, block_at(2))
+        along("raf", block_at(2), -1)
+        along("second", block_at(2, 1), -2)
+        f_copies[-2].wait_recv()
+        along("over", block_at(-2, plane=1 - zl), 1)
+        f_copies[2].wait_recv()
+        along("revo", block_at(2, plane=1 - zl), -1)
         g_copies["first"].wait_recv()
-        across(block_at(4, 0))
+        across(4, block_at(4, 0))
         g_copies["second"].wait_recv()
-        across(block_at(4, 1))
-    for copy in f_copies.values():
-        copy.wait_recv()
+        across(-4, block_at(4, 1))
+        for name in (1, -1, "near", "raen", "far", "raf", "over", "revo"):
+            g_copies[name].wait_recv()
+        f_copies[4].wait_recv()
+        f_copies[-4].wait_recv()
+    else:
+        f_copies[0].wait_recv()
 
     product = dot(kva[...], hidden_v[...], TT)
     for k in range(2):
@@ -371,7 +402,7 @@
             w_f32[k, j] = product[at : at + block].reshape(w_f32.shape[2:])
     csend[...] = w_f32[1 - core].astype(BF16)
     c_copies = {}
-    order = [0] if ny == 1 else [4, 3, 5, 2, 6, 1, 7, 0]
+    order = [0] if ny == 1 else [4, 3, 5, 1, 7, 2, 6, 0]
     for d in order:
         to = (y + d) % ny
         c_copies[d] = remote(csend.at[to], crecv.at[to], cs_sem, cr_sem.at[d], core_peer)
@@ -384,7 +415,7 @@
         own_c[owner] = own_c[owner] + crecv[owner].astype(F32)
 
     y_ring = Ring(y_peer, ysend, yrecv, ys_sem, yr_sem, (block // 8 + 1) // 2)
-    mine_c = y_ring.reduce(ny, y, from_core, own_c)
+    mine_c = y_ring.reduce(ny, y, from_core, own_c, False)
     hidden_out[...] = dot(down_p[...], kva[...], NT).astype(BF16)
     total = y_ring.collect(ny, mine_c)
     acc_c[...] = total.reshape(acc_c.shape)
@@ -403,18 +434,20 @@
         result = result + hi_recv[d, 0:own, :].astype(F32)
     weight_out[...] = result
 
-    remote(zsend, zrecv, zs_sem, zr_sem.at[0], z_peer).wait_send()
+    def sent(ref, count, sem, recv_sem):
+        part = ref.at[pl.ds(0, count)]
+        remote(part, part, sem, recv_sem.at[0], z_peer).wait_send()
+
+    sent(zsend, min(nx, 6), zs_sem, zr_sem)
     x_ring.finish(nx)
     if nx > 1:
-        sent = kva.at[pl.ds(0, 7 * ROWS), :]
-        remote(sent, sent, gs_sem, gr_sem.at[0], x_peer[1]).wait_send()
-    passed = kva.at[pl.ds(0, nx * ROWS), :]
-    remote(passed, passed, fs_sem, fr_sem.at[0], z_peer).wait_send()
+        sent(zsend, 2, ps_sem, pr_sem)
+        sent(kva, 11 * ROWS, gs_sem, gr_sem)
+    sent(kva, min(nx, 4) * ROWS, fs_sem, fr_sem)
     remote(csend, crecv, cs_sem, cr_sem.at[0], core_peer).wait_send()
     y_ring.finish(ny)
     if nzh > 1:
-        sent = pl.ds(1, nzh - 1)
-        remote(hi_send.at[sent], hi_recv.at[sent], hs_sem, hr_sem.at[1], core_peer).wait_send()
+        sent(hi_send, nzh - 1, hs_sem, hr_sem)
 
 
 def on_device(lay, *args):
@@ -444,6 +477,8 @@
         pltpu.VMEM((nx, TILES, 16, 128), F32),
         pltpu.VMEM((nx, TILES, 16, 128), BF16),
         pltpu.VMEM((nx, TILES, 16, 128), BF16),
+        pltpu.VMEM((2, TILES, 16, 128), BF16),
+        pltpu.VMEM((TILES, 16, 128), BF16),
         pltpu.VMEM((7, TILES, 16, 128), BF16),
         pltpu.VMEM((7, TILES, 16, 128), BF16),
         pltpu.VMEM((TILES, 16, 128), F32),
@@ -462,11 +497,13 @@
         dma,
         dma((8,)),
         dma,
+        dma((2,)),
+        dma,
         dma((8,)),
         dma,
-        dma((8,)),
-        dma,
-        dma((9,)),
+        dma((12,)),
+        dma,
+        dma((5,)),
         dma,
         dma((8,)),
         dma,

time: 62.8 us -> 62.3 us (level)
  no operation moved by 1% of the time
where the time goes in v3:
time: 62.3 us; the launch traced here: 62.1 us
  Pallas kernels  60.1 us (96%)
  local copies, waits for them, and re-layouts  1.38 us (2%)
  between operations  0.64 us (1%)
    pallas_call x1, Pallas kernels, on_device(): pl.pallas_call(functools.partial(kernel, lay), out_shape=(pltpu.VMEM((col...  60.1 us
    unnamed x2, local copies, waits for them, and re-layouts  1.38 us

profile of v3, /device:TPU:1, one launch (start us, length us, event | category | flops | bytes accessed | tf_op | source)
XLA Modules:
  0.0 62.1 jit_solution(6223937442213539183)
XLA Ops:
  0.6 60.1 %latent_backward.1 = (bf16[448,512]{1,0:T(8,128)(2,1)S(1)}, f32[9,448]{1,0:T(8,128)S(1)}) custom-call(bf16[512,1024]{1,0:T(8,128)(2,1)} %key_hbm.1, bf16[512,1024]{1,0:T(8,128)(2,1)} %value_hbm.1, bf16[512,512]{1,0:T(8,128)(2,1)} %rope_hbm.1, bf16[512,1024]{1,0:T(8,128)(2,1)} %key_lift_hbm.1, bf16[512,1024]{1,0:T(8,128)(2,1)} %value_lift_hbm.1, ...), custom_call_target="tpu_custom_call" | custom-call | tf_op jit(solution)/shard_map/latent_backward/pallas_call | solution.py:514
  60.8 0.8 %copy.14 = bf16[512,448]{0,1:T(8,128)(2,1)} copy(bf16[512,448]{0,1:T(8,128)(2,1)S(1)} %bitcast.3) | data formatting | bytes 917504
  61.5 0.6 copy.15

commit v4 on v3

--- a/solution.py
+++ b/solution.py
@@ -82,7 +82,7 @@
         whole[rows] = whole[rows] + self.recv[2, rows].astype(F32)
         self.put(name, term_ref[index])
 
-    def reduce(self, size, me, ready, term_ref, near_first):
+    def reduce(self, size, me, ready, term_ref, near_left):
         def at(offset):
             return (me + offset + size) % size
 
@@ -92,13 +92,10 @@
 
         if size == 1:
             return term(0)
-        if near_first:
-            self.put("one", term(1))
-            self.put("eno", term(-1))
         self.put_opposite(term(4))
         self.put("far", term(3))
         self.put("raf", term(-3))
-        if not near_first:
+        if not near_left:
             self.put("one", term(1))
             self.put("eno", term(-1))
         ready(2, at(2))
@@ -282,6 +279,23 @@
         for i, tile in tiles(terms, ropes, chunk):
             own_a[chunk, i] = tile
 
+    def from_z(offset, owner):
+        if offset == 3:
+            near_sum = zsend[x].astype(F32)
+            for slot in p_copies:
+                p_copies[slot].wait_recv()
+                near_sum = near_sum + precv[slot].astype(F32)
+            zsum[...] = near_sum.astype(BF16)
+            z_copies[0] = remote(zsum, zrecv.at[x], zs_sem, zr_sem.at[0], z_peer)
+            z_copies[0].start()
+        z_copies[offset].wait_recv()
+        own_a[owner] = own_a[owner] + zrecv[owner].astype(F32)
+
+    x_ring = Ring(x_peer, xsend, xrecv, xs_sem, xr_sem, 5, direct=True)
+    if nx > 1:
+        x_ring.put("one", own_a[(x + 1) % nx])
+        x_ring.put("eno", own_a[(x + nx - 1) % nx])
+
     for copy in fourth:
         copy.wait()
     block, own = lay.block, lay.own
@@ -316,21 +330,6 @@
     values = latent_v[...].astype(F32)
     inverse = lax.rsqrt(jnp.mean(values * values, axis=1, keepdims=True) + 1e-06)
 
-    def from_z(offset, owner):
-        if offset in (1, 7):
-            return
-        if offset == 3:
-            near_sum = zsend[x].astype(F32)
-            for slot in p_copies:
-                p_copies[slot].wait_recv()
-                near_sum = near_sum + precv[slot].astype(F32)
-            zsum[...] = near_sum.astype(BF16)
-            z_copies[0] = remote(zsum, zrecv.at[x], zs_sem, zr_sem.at[0], z_peer)
-            z_copies[0].start()
-        z_copies[offset].wait_recv()
-        own_a[owner] = own_a[owner] + zrecv[owner].astype(F32)
-
-    x_ring = Ring(x_peer, xsend, xrecv, xs_sem, xr_sem, 5, direct=True)
     mine_a = x_ring.reduce(nx, x, from_z, own_a, True)
     acc_a[...] = x_ring.collect(nx, mine_a)
 
@@ -351,6 +350,13 @@
         head = (zl if plane is None else plane) * nx + (x + offset + nx) % nx
         first, size = (0, ROWS) if part is None else (part * ROWS // 2, ROWS // 2)
         return kva.at[pl.ds(pl.multiple_of(head * ROWS + first, size), size), :]
+
+    def keep_product(product, add=False):
+        for k in range(2):
+            for j in range(ny):
+                at = (k * ny + j) * block
+                piece = product[at : at + block].reshape(w_f32.shape[2:])
+                w_f32[k, j] = w_f32[k, j] + piece if add else piece
 
     g_copies, f_copies = {}, {}
 
@@ -388,18 +394,18 @@
         across(4, block_at(4, 0))
         g_copies["second"].wait_recv()
         across(-4, block_at(4, 1))
-        for name in (1, -1, "near", "raen", "far", "raf", "over", "revo"):
+        for name in (1, -1, "far", "raf"):
+            g_copies[name].wait_recv()
+        keep_product(dot(kva[mine, :], hidden_v[:, mine], TT))
+        for name in ("near", "raen", "over", "revo"):
             g_copies[name].wait_recv()
         f_copies[4].wait_recv()
         f_copies[-4].wait_recv()
     else:
+        keep_product(dot(kva[mine, :], hidden_v[:, mine], TT))
         f_copies[0].wait_recv()
 
-    product = dot(kva[...], hidden_v[...], TT)
-    for k in range(2):
-        for j in range(ny):
-            at = (k * ny + j) * block
-            w_f32[k, j] = product[at : at + block].reshape(w_f32.shape[2:])
+    keep_product(dot(kva[theirs, :], hidden_v[:, theirs], TT), add=True)
     csend[...] = w_f32[1 - core].astype(BF16)
     c_copies = {}
     order = [0] if ny == 1 else [4, 3, 5, 1, 7, 2, 6, 0]
@@ -448,6 +454,17 @@
     y_ring.finish(ny)
     if nzh > 1:
         sent(hi_send, nzh - 1, hs_sem, hr_sem)
+
+
+def hand_over(hidden_ref, weight_ref, hidden_out, weight_out, sem):
+    copies = [
+        pltpu.make_async_copy(hidden_ref, hidden_out, sem.at[0]),
+        pltpu.make_async_copy(weight_ref, weight_out, sem.at[1]),
+    ]
+    for copy in copies:
+        copy.start()
+    for copy in copies:
+        copy.wait()
 
 
 def on_device(lay, *args):
@@ -525,6 +542,18 @@
         ),
         name="latent_backward",
     )(key, value, rope, key_lift, value_lift, latent, gain.reshape(1, -1), docs, hidden, down)
+    hidden_grad, weight_grad = pl.pallas_call(
+        hand_over,
+        out_shape=(
+            jax.ShapeDtypeStruct((cols, lay.seq), BF16),
+            jax.ShapeDtypeStruct((lay.own, cols), F32),
+        ),
+        in_specs=[any_spec] * 2,
+        out_specs=(any_spec,) * 2,
+        scratch_shapes=[dma((2,))],
+        compiler_params=pltpu.CompilerParams(vmem_limit_bytes=4 * 1024 * 1024),
+        name="hand_over",
+    )(hidden_grad, weight_grad)
     return hidden_grad.T, weight_grad
 
 

time: 62.3 us -> 61.7 us (level)
  local copies, waits for them, and re-layouts: 1.38 us -> 0 us
  Pallas kernels: 60.1 us -> 60.9 us
    unnamed x2 -> x0, local copies, waits for them, and re-layouts: 1.38 us -> none
    pallas_call x0 -> x1, Pallas kernels: none -> 0.79 us  [on_device(): pl.pallas_call(hand_over, out_shape=(jax.ShapeDtypeStruct((cols, lay.seq)...]
where the time goes in v4:
time: 61.7 us; the launch traced here: 61.6 us
  Pallas kernels  60.9 us (99%)
  between operations  0.64 us (1%)
    pallas_call x1, Pallas kernels, on_device(): pl.pallas_call(functools.partial(kernel, lay), out_shape=(pltpu.VMEM((col...  60.1 us

profile of v4, /device:TPU:1, one launch (start us, length us, event | category | flops | bytes accessed | tf_op | source)
XLA Modules:
  0.0 61.6 jit_solution(14341135343312901902)
XLA Ops:
  0.6 60.1 %latent_backward.1 = (bf16[448,512]{1,0:T(8,128)(2,1)S(1)}, f32[9,448]{1,0:T(8,128)S(1)}) custom-call(bf16[512,1024]{1,0:T(8,128)(2,1)} %key_hbm.1, bf16[512,1024]{1,0:T(8,128)(2,1)} %value_hbm.1, bf16[512,512]{1,0:T(8,128)(2,1)} %rope_hbm.1, bf16[512,1024]{1,0:T(8,128)(2,1)} %key_lift_hbm.1, bf16[512,1024]{1,0:T(8,128)(2,1)} %value_lift_hbm.1, ...), custom_call_target="tpu_custom_call" | custom-call | tf_op jit(solution)/shard_map/latent_backward/pallas_call | solution.py:531
  60.8 0.8 %hand_over.1 = (bf16[448,512]{1,0:T(8,128)(2,1)}, f32[9,448]{1,0:T(8,128)}) custom-call(bf16[448,512]{1,0:T(8,128)(2,1)S(1)} %get-tuple-element.6.hidden_ref, f32[9,448]{1,0:T(8,128)S(1)} %get-tuple-element.7.weight_ref), custom_call_target="tpu_custom_call" | custom-call | tf_op jit(solution)/shard_map/hand_over/pallas_call | solution.py:545
